TPU v7x, 32 devices: a whole 2x2x4 slice. The times are simulated.
32 devices in a mesh: dp: 4 (over z), group: 8 (over y, x, core).
Axes of the slice: x: 2, y: 2, z: 4, core: 2. Of those that a mesh axis runs over, the one named last changes fastest.
Arguments:
- query: bfloat16 [4096, 4096], P(('dp', 'group')), may hold values from -6 to 6
- comp_key: bfloat16 [4096, 512], P(('dp', 'group')), may hold values from -6 to 6
- comp_value: bfloat16 [4096, 512], P(('dp', 'group')), may hold values from -6 to 6
- prompt_key: bfloat16 [128, 512], P(('dp', 'group')), may hold values from -6 to 6
- prompt_value: bfloat16 [128, 512], P(('dp', 'group')), may hold values from -6 to 6
- d_out: bfloat16 [4096, 4096], P(('dp', 'group')), may hold values from -6 to 6
- q_gain: float32 [128], replicated, may hold values from 0.5 to 1.5
- k_gain: float32 [128], replicated, may hold values from 0.5 to 1.5
- lengths: int32 [32], P(('dp', 'group')), may hold values from 1 to 128, 2560 in all
Outputs:
- d_query: bfloat16 [4096, 4096], P(('dp', 'group'))
- d_comp_key: bfloat16 [4096, 512], P(('dp', 'group'))
- d_comp_value: bfloat16 [4096, 512], P(('dp', 'group'))
- d_prompt_key: bfloat16 [128, 512], P(('dp', 'group'))
- d_prompt_value: bfloat16 [128, 512], P(('dp', 'group'))
- d_q_gain: float32 [128], replicated
- d_k_gain: float32 [128], replicated
Inputs may be any that keep to these rules, and one draw needn't show every extreme that they name: `lengths`: each entry is the live slots of one completion, at most 128; some completion has exactly 128.
All inputs are finite; a program needn't handle non-finite values. No bound on the sum of `lengths` on one device may be relied on, other than what follows from the above.
Results may differ from a plain program's by a relative error of at most 0.025.
Values may be sent and summed in bfloat16 or wider, within the bound.
A program may use at most 64 MiB of HBM per device.

v0:
```python
import jax
import jax.numpy as jnp
from jax import lax
from jax.sharding import PartitionSpec as P

HD = 128
HQ = 32
HK = 4
EPS = 1e-06


def normalize(vectors, gain):
    wide = vectors.astype(jnp.float32)
    inverse = lax.rsqrt(jnp.mean(wide * wide, axis=-1, keepdims=True) + EPS)
    unit = wide * inverse
    return ((unit * gain).astype(jnp.bfloat16), unit, inverse)


def norm_back(grad, unit, inverse, gain):
    scaled = grad * gain
    back = inverse * (scaled - unit * jnp.mean(scaled * unit, axis=-1, keepdims=True))
    return (back, jnp.sum((grad * unit).reshape(-1, unit.shape[-1]), axis=0))


def head_grads(query_head, key_head, value_head, grad_head, visible, scale):
    scores = (
        jnp.einsum("cgd,kd->gck", query_head, key_head, preferred_element_type=jnp.float32) * scale
    )
    expo = jnp.where(visible[None], jnp.exp(scores), 0.0)
    totals = jnp.sum(expo, axis=-1, keepdims=True)
    rounded = (expo / totals).astype(jnp.bfloat16)
    output = jnp.einsum("gck,kd->cgd", rounded, value_head, preferred_element_type=jnp.float32)
    delta = jnp.transpose(jnp.sum(grad_head.astype(jnp.float32) * output, axis=-1))[..., None]
    dprob = jnp.einsum("cgd,kd->gck", grad_head, value_head, preferred_element_type=jnp.float32)
    dscore = (expo / totals * (dprob - delta)).astype(jnp.bfloat16)
    dquery = jnp.einsum("gck,kd->cgd", dscore, key_head, preferred_element_type=jnp.float32) * scale
    dkey = jnp.einsum("gck,cgd->kd", dscore, query_head, preferred_element_type=jnp.float32) * scale
    dvalue = jnp.einsum("gck,cgd->kd", rounded, grad_head, preferred_element_type=jnp.float32)
    return (dquery, dkey, dvalue, totals, delta)


def local(query, comp_key, comp_value, prompt_key, prompt_value, d_out, q_gain, k_gain, lengths):
    count = query.shape[0]
    shard = prompt_key.shape[0]
    groups = HQ // HK
    scale = HD ** (-0.5)
    qnorm, qunit, qinv = normalize(query.reshape(count, HQ, HD), q_gain)
    cnorm, cunit, cinv = normalize(comp_key.reshape(count, HK, HD), k_gain)
    pnorm, punit, pinv = normalize(prompt_key.reshape(shard, HK, HD), k_gain)
    pkeys, pvalues = (
        lax.all_gather(pnorm.reshape(shard, HK * HD), "group", axis=0, tiled=True),
        lax.all_gather(prompt_value, "group", axis=0, tiled=True),
    )
    prompt_len = pkeys.shape[0]
    keys = jnp.concatenate([pkeys, cnorm.reshape(count, HK * HD)], axis=0).reshape(-1, HK, HD)
    values = jnp.concatenate([pvalues, comp_value], axis=0).reshape(-1, HK, HD)
    slots = lax.broadcasted_iota(jnp.int32, (count, count), 0)
    others = lax.broadcasted_iota(jnp.int32, (count, count), 1)
    visible = jnp.concatenate([jnp.ones((count, prompt_len), bool), others <= slots], axis=1)
    live = (jnp.arange(count, dtype=jnp.int32) < lengths[0])[:, None]
    masked = jnp.where(live, d_out, jnp.zeros_like(d_out))
    query_four = qnorm.reshape(count, HK, groups, HD)
    grad_four = masked.reshape(count, HK, groups, HD)
    results = [
        head_grads(
            query_four[:, head], keys[:, head], values[:, head], grad_four[:, head], visible, scale
        )
        for head in range(HK)
    ]
    dquery = jnp.stack([item[0] for item in results], axis=1).reshape(count, HQ, HD)
    dkey_all = jnp.stack([item[1] for item in results], axis=1)
    dvalue_all = jnp.stack([item[2] for item in results], axis=1)
    term = jnp.concatenate(
        [
            dkey_all[:prompt_len].reshape(prompt_len, HK * HD),
            dvalue_all[:prompt_len].reshape(prompt_len, HK * HD),
        ],
        axis=1,
    )
    summed = lax.psum_scatter(
        term.astype(jnp.bfloat16), "group", scatter_dimension=0, tiled=True
    ).astype(jnp.float32)
    dkey_comp = dkey_all[prompt_len:]
    dvalue_comp = dvalue_all[prompt_len:]
    dkey_prompt = summed[:, : HK * HD].reshape(shard, HK, HD)
    dvalue_prompt = summed[:, HK * HD :]
    dq, gain_query = norm_back(dquery, qunit, qinv, q_gain)
    dck, gain_comp = norm_back(dkey_comp, cunit, cinv, k_gain)
    dpk, gain_prompt = norm_back(dkey_prompt, punit, pinv, k_gain)
    gain_query, gain_key = lax.psum((gain_query, gain_comp + gain_prompt), ("dp", "group"))
    return (
        dq.reshape(count, HQ * HD).astype(jnp.bfloat16),
        dck.reshape(count, HK * HD).astype(jnp.bfloat16),
        dvalue_comp.reshape(count, HK * HD).astype(jnp.bfloat16),
        dpk.reshape(shard, HK * HD).astype(jnp.bfloat16),
        dvalue_prompt.astype(jnp.bfloat16),
        gain_query,
        gain_key,
    )


def solution(mesh):
    return jax.shard_map(
        local,
        mesh=mesh,
        in_specs=(
            P(("dp", "group"), None),
            P(("dp", "group"), None),
            P(("dp", "group"), None),
            P(("dp", "group"), None),
            P(("dp", "group"), None),
            P(("dp", "group"), None),
            P(),
            P(),
            P(("dp", "group")),
        ),
        out_specs=(
            P(("dp", "group"), None),
            P(("dp", "group"), None),
            P(("dp", "group"), None),
            P(("dp", "group"), None),
            P(("dp", "group"), None),
            P(),
            P(),
        ),
        check_vma=False,
    )
```

profile of v0, /device:TPU:0, one launch (start us, length us, event | category | flops | bytes accessed | tf_op | source)
XLA Modules:
  0.0 174.6 jit_solution(7659037354188881462)
XLA Ops:
  7.2 0.6 iota_compare_fusion
  7.8 0.7 broadcast_bitcast_fusion.3
  8.5 0.7 reshape.176
  9.9 0.6 copy-done.32
  10.5 0.7 fusion.87
  11.2 10.6 %all-gather = bf16[8,4,512]{2,1,0:T(4,128)(2,1)S(1)} all-gather(bf16[1,4,512]{2,1,0:T(4,128)(2,1)S(1)} %fusion.87), channel_id=1, replica_groups=mesh['dp'=4,'group'=8] {'group'}, dimensions={0}, use_global_device_ids=true | all-gather | bytes 36864 | tf_op jit(solution)/shard_map/all_gather | solution.py:51
  21.8 0.6 copy.94
  22.4 1.0 copy.92
  23.8 0.7 copy.91
  24.7 0.8 add_rsqrt_fusion
  26.0 1.3 concatenate.21
  27.3 1.3 fusion.81
  28.6 1.4 multiply_convert_fusion
  30.0 2.0 %fusion.52 = f32[8,128,160]{1,2,0:T(8,128)} fusion(pred[128,160]{0,1:T(8,128)(4,1)} %concatenate.21, bf16[128,4,8,128]{3,0,2,1:T(8,128)(2,1)S(1)} %multiply_convert_fusion, bf16[128,4,128]{2,0,1:T(8,128)(2,1)S(1)} %copy.95, bf16[32,4,128]{2,0,1:T(8,128)(2,1)} %copy.94), kind=kOutput, calls=%fused_computation.88 | convolution fusion | flops 42517664 | bytes 1101824 | tf_op jit(solution)/shard_map/div | solution.py:35
  32.0 1.9 %fusion.54 = f32[8,128,160]{1,2,0:T(8,128)} fusion(pred[128,160]{0,1:T(8,128)(4,1)} %concatenate.21, bf16[128,4,8,128]{3,0,2,1:T(8,128)(2,1)S(1)} %multiply_convert_fusion, bf16[128,4,128]{2,0,1:T(8,128)(2,1)S(1)} %copy.95, bf16[32,4,128]{2,0,1:T(8,128)(2,1)} %copy.94), kind=kOutput, calls=%fused_computation.90 | convolution fusion | flops 42517664 | bytes 1101824 | tf_op jit(solution)/shard_map/div | solution.py:35
  33.9 2.0 %fusion.56 = f32[8,128,160]{1,2,0:T(8,128)} fusion(pred[128,160]{0,1:T(8,128)(4,1)} %concatenate.21, bf16[128,4,8,128]{3,0,2,1:T(8,128)(2,1)S(1)} %multiply_convert_fusion, bf16[128,4,128]{2,0,1:T(8,128)(2,1)S(1)} %copy.95, bf16[32,4,128]{2,0,1:T(8,128)(2,1)} %copy.94), kind=kOutput, calls=%fused_computation.92 | convolution fusion | flops 42517664 | bytes 1101824 | tf_op jit(solution)/shard_map/div | solution.py:35
  37.1 9.3 %all-gather.1 = bf16[8,4,512]{2,1,0:T(4,128)(2,1)S(1)} all-gather(bf16[1,4,512]{2,1,0:T(4,128)(2,1)} %bitcast.375), channel_id=1, replica_groups=mesh['dp'=4,'group'=8] {'group'}, dimensions={0}, use_global_device_ids=true | all-gather | bytes 36864 | tf_op jit(solution)/shard_map/all_gather | solution.py:52
  46.3 0.9 pad_maximum_fusion.2
  47.3 0.9 fusion.122
  48.2 2.3 %copy.98 = bf16[128,4096]{0,1:T(8,128)(2,1)} copy(bf16[128,4096]{1,0:T(8,128)(2,1)} %param.14) | data formatting | bytes 2097152 | tf_op args[5]
  50.5 1.3 broadcast_select_fusion
  51.8 1.0 fusion.121
  52.8 1.8 %copy.133 = bf16[128,1,8,128]{3,0,2,1:T(8,128)(2,1)} copy(bf16[128,1,8,128]{0,3,2,1:T(8,128)(2,1)} %get-tuple-element.38) | data formatting | bytes 524288
  54.6 1.8 %copy.137 = bf16[128,1,8,128]{3,0,2,1:T(8,128)(2,1)} copy(bf16[128,1,8,128]{0,3,2,1:T(8,128)(2,1)} %get-tuple-element.39) | data formatting | bytes 524288
  56.4 1.8 %copy.135 = bf16[128,1,8,128]{3,0,2,1:T(8,128)(2,1)} copy(bf16[128,1,8,128]{0,3,2,1:T(8,128)(2,1)} %get-tuple-element.40) | data formatting | bytes 524288
  58.2 1.8 %copy.139 = bf16[128,1,8,128]{3,0,2,1:T(8,128)(2,1)} copy(bf16[128,1,8,128]{0,3,2,1:T(8,128)(2,1)} %get-tuple-element.41) | data formatting | bytes 524288
  60.0 2.1 %fusion.50 = f32[8,128,160]{1,2,0:T(8,128)} fusion(bf16[160,128,1]{1,0,2:T(8,128)(2,1)} %fusion.81, pred[128,160]{0,1:T(8,128)(4,1)} %concatenate.21, bf16[128,4,8,128]{3,0,2,1:T(8,128)(2,1)} %copy-done.6), kind=kOutput, calls=%fused_computation.86 | convolution fusion | flops 42435744 | bytes 978944 | tf_op jit(solution)/shard_map/div | solution.py:35
  62.1 1.5 convolution_bitcast_fusion.8
  63.6 1.7 fusion.37
  65.3 1.1 fusion.36
  71.2 0.6 pad_maximum_fusion.3
  71.9 1.3 broadcast_bitcast_fusion
  73.2 2.1 %fusion.29 = f32[128,1,8,128]{3,0,2,1:T(8,128)} fusion(bf16[160,128,1]{1,0,2:T(8,128)(2,1)} %fusion.81, bf16[8,128,160]{1,2,0:T(8,128)(2,1)} %copy-done.8), kind=kOutput, calls=%fused_computation.51 | convolution fusion | flops 42074112 | bytes 892928 | tf_op jit(solution)/shard_map/gck,kd->cgd/dot_general | solution.py:36
  75.3 2.2 %fusion.30 = f32[128,1,8,128]{3,0,2,1:T(8,128)} fusion(bf16[8,128,160]{1,2,0:T(8,128)(2,1)} %copy-done.9, bf16[128,4,128]{2,0,1:T(8,128)(2,1)S(1)} %copy.95, bf16[32,4,128]{2,0,1:T(8,128)(2,1)} %copy.94), kind=kOutput, calls=%fused_computation.53 | convolution fusion | flops 42156032 | bytes 1015808 | tf_op jit(solution)/shard_map/gck,kd->cgd/dot_general | solution.py:36
  77.5 1.2 fusion.31
  78.7 0.7 maximum_convert_fusion
  79.4 1.1 fusion.32
  81.2 3.6 %multiply_reduce_fusion = (f32[128,4,8]{0,2,1:T(8,128)S(1)}, f32[128,4,8,128]{3,0,2,1:T(8,128)}) fusion(f32[128,4,8,128]{3,0,2,1:T(8,128)S(1)} %copy.96, f32[128]{0:T(128)S(1)} %copy-done.45, f32[128,4,8]{0,2,1:T(8,128)S(1)} %get-tuple-element.49, f32[128,1,8,128]{3,0,2,1:T(8,128)} %fusion.29, f32[128,1,8,128]{3,0,2,1:T(8,128)} %fusion.30, ...), kind=kLoop, calls=%fused_computation.11 | loop fusion | flops 3665920 | bytes 6324736 | tf_op jit(solution)/shard_map/reduce_sum | solution.py:21
  84.8 2.0 %copy.114 = f32[128,4,8,128]{0,3,2,1:T(8,128)S(1)} copy(f32[128,4,8,128]{3,0,2,1:T(8,128)} %get-tuple-element.37) | data formatting | bytes 4194304 | tf_op jit(solution)/shard_map/stack | solution.py:70
  86.8 2.2 %fusion.4 = (f32[4096]{0:T(1024)S(1)}, bf16[128,4096]{0,1:T(8,128)(2,1)}) fusion(f32[128,4,8,128]{0,3,2,1:T(8,128)S(1)} %copy.114, bf16[128,4096]{0,1:T(8,128)(2,1)S(1)} %copy-done.1, f32[128,4,8]{0,2,1:T(8,128)S(1)} %get-tuple-element.49, f32[128,32]{0,1:T(8,128)S(1)} %multiply_bitcast_fusion, f32[4096]{0:T(1024)S(1)} %copy-done.35, f32[128,32]{0,1:T(8,128)S(1)} %copy-done.34), kind=kLoop, calls=%fused_computation.8 | loop fusion | flops 5238784 | bytes 4276224 | tf_op jit(solution)/shard_map/reduce_sum | solution.py:22
  89.3 0.8 copy.123
  90.2 0.8 copy.122
  91.0 2.3 %copy.121 = bf16[128,4096]{1,0:T(8,128)(2,1)} copy(bf16[128,4096]{0,1:T(8,128)(2,1)} %get-tuple-element.35) | data formatting | bytes 2097152
  93.3 0.6 dynamic-slice
  94.5 30.9 %all-reduce.5.cloned.1.call-done = bf16[32,1024]{1,0:T(8,128)(2,1)} async-done(((bf16[32,1024]{1,0:T(8,128)(2,1)}), bf16[32,1024]{1,0:T(8,128)(2,1)}) %all-reduce.5.cloned.1.call-update) | async-done | bytes 65552
  125.4 1.4 fusion.123
  127.2 39.3 %all-reduce.2 = (f32[128]{0:T(128)}, f32[128]{0:T(128)}) all-reduce(f32[128]{0:T(128)S(1)} %bitcast_reduce_fusion.1, f32[128]{0:T(128)S(1)} %add.48), channel_id=1, replica_groups=mesh['dp'=4,'group'=8] {'dp','group'}, use_global_device_ids=true, to_apply=%region_17.18 | all-reduce | flops 256 | bytes 2048 | tf_op jit(solution)/shard_map/psum | solution.py:90
  166.5 1.3 fusion.86
  (142 shorter events, 8.2 us)
Async XLA Ops:
  7.2 16.6 %copy-start.14 = (bf16[128,4096]{1,0:T(8,128)(2,1)S(1)}, bf16[128,4096]{1,0:T(8,128)(2,1)}, u32[]{:S(2)}) copy-start(bf16[128,4096]{1,0:T(8,128)(2,1)} %param.9) | copy-start | bytes 3145732
  7.2 118.3 %all-reduce.5.cloned.1.call-start = ((), (), s32[]{:S(2)}) async-start(), calls=%async_computation | async-start | bytes 131072
  8.5 16.2 %copy-start.39 = (f32[512]{0:T(512)}, f32[512]{0:T(512)S(1)}, u32[]{:S(2)}) copy-start(f32[512]{0:T(512)S(1)} %broadcast_bitcast_fusion.3) | copy-start | bytes 6148
  9.2 0.6 copy-start.30
  9.9 0.6 copy-start.32
  23.5 2.0 %copy-start.37 = (f32[128,4]{0,1:T(4,128)}, f32[128,4]{0,1:T(4,128)S(1)}, u32[]{:S(2)}) copy-start(f32[128,4]{0,1:T(4,128)S(1)} %add_rsqrt_fusion.1) | copy-start | bytes 6148
  24.4 1.6 copy-start
  30.0 3.9 %copy-start.6 = (bf16[128,4,8,128]{3,0,2,1:T(8,128)(2,1)}, bf16[128,4,8,128]{3,0,2,1:T(8,128)(2,1)S(1)}, u32[]{:S(2)}) copy-start(bf16[128,4,8,128]{3,0,2,1:T(8,128)(2,1)S(1)} %multiply_convert_fusion) | copy-start | bytes 3145732
  62.1 3.2 %copy-start.5 = (f32[8,128,160]{1,2,0:T(8,128)S(1)}, f32[8,128,160]{1,2,0:T(8,128)}, u32[]{:S(2)}) copy-start(f32[8,128,160]{1,2,0:T(8,128)} %fusion.50) | copy-start | bytes 1966084
  62.1 4.4 %copy-start.7 = (bf16[128,4,8,128]{3,0,2,1:T(8,128)(2,1)S(1)}, bf16[128,4,8,128]{3,0,2,1:T(8,128)(2,1)}, u32[]{:S(2)}) copy-start(bf16[128,4,8,128]{3,0,2,1:T(8,128)(2,1)} %copy-done.6) | copy-start | bytes 3145732
  62.1 4.6 %copy-start.4 = (f32[8,128,160]{1,2,0:T(8,128)S(1)}, f32[8,128,160]{1,2,0:T(8,128)}, u32[]{:S(2)}) copy-start(f32[8,128,160]{1,2,0:T(8,128)} %fusion.52) | copy-start | bytes 1966084
  63.6 7.2 %copy-start.19 = (bf16[160,1,128]{2,0,1:T(8,128)(2,1)}, bf16[160,1,128]{2,0,1:T(8,128)(2,1)S(1)}, u32[]{:S(2)}) copy-start(bf16[160,1,128]{2,0,1:T(8,128)(2,1)S(1)} %convolution_bitcast_fusion.8) | copy-start | bytes 122884
  63.6 3.4 %copy-start.17 = (bf16[128,1,8,128]{3,0,2,1:T(8,128)(2,1)S(1)}, bf16[128,1,8,128]{3,0,2,1:T(8,128)(2,1)}, u32[]{:S(2)}) copy-start(bf16[128,1,8,128]{3,0,2,1:T(8,128)(2,1)} %copy.137) | copy-start | bytes 786436
  63.6 3.4 %copy-start.29 = (bf16[160,1,128]{2,1,0:T(2,128)(2,1)S(1)}, bf16[160,1,128]{2,1,0:T(2,128)(2,1)}, u32[]{:S(2)}) copy-start(bf16[160,1,128]{2,1,0:T(2,128)(2,1)} %get-tuple-element.43) | copy-start | bytes 122884
  66.5 1.6 copy-start.8
  66.7 1.3 copy-start.3
  67.0 3.7 %copy-start.21 = (bf16[160,1,128]{2,0,1:T(8,128)(2,1)}, bf16[160,1,128]{2,0,1:T(8,128)(2,1)S(1)}, u32[]{:S(2)}) copy-start(bf16[160,1,128]{2,0,1:T(8,128)(2,1)S(1)} %convolution_bitcast_fusion.9) | copy-start | bytes 122884
  67.0 1.4 copy-start.16
  67.0 1.4 copy-start.28
  67.8 1.6 copy-start.9
  68.1 1.3 copy-start.2
  68.3 2.4 %copy-start.23 = (bf16[160,1,128]{2,0,1:T(8,128)(2,1)}, bf16[160,1,128]{2,0,1:T(8,128)(2,1)S(1)}, u32[]{:S(2)}) copy-start(bf16[160,1,128]{2,0,1:T(8,128)(2,1)S(1)} %convolution_bitcast_fusion.10) | copy-start | bytes 122884
  68.3 1.3 copy-start.15
  68.4 1.3 copy-start.27
  69.1 1.6 copy-start.10
  69.7 1.5 copy-start.25
  70.4 0.7 copy-start.12
  70.4 7.1 %copy-start.18 = (bf16[32,4,128]{2,0,1:T(8,128)(2,1)S(1)}, bf16[32,4,128]{2,0,1:T(8,128)(2,1)}, u32[]{:S(2)}) copy-start(bf16[32,4,128]{2,0,1:T(8,128)(2,1)} %copy.94) | copy-start | bytes 98308
  71.1 6.4 %copy-start.11 = (bf16[8,128,160]{1,2,0:T(8,128)(2,1)S(1)}, bf16[8,128,160]{1,2,0:T(8,128)(2,1)}, u32[]{:S(2)}) copy-start(bf16[8,128,160]{1,2,0:T(8,128)(2,1)} %copy-done.10) | copy-start | bytes 983044
  71.2 8.2 %copy-start.13 = (bf16[8,128,160]{1,2,0:T(8,128)(2,1)S(1)}, bf16[8,128,160]{1,2,0:T(8,128)(2,1)}, u32[]{:S(2)}) copy-start(bf16[8,128,160]{1,2,0:T(8,128)(2,1)} %copy-done.12) | copy-start | bytes 983044
  71.8 6.8 %copy-start.20 = (bf16[160,1,128]{2,0,1:T(8,128)(2,1)S(1)}, bf16[160,1,128]{2,0,1:T(8,128)(2,1)}, u32[]{:S(2)}) copy-start(bf16[160,1,128]{2,0,1:T(8,128)(2,1)} %copy-done.19) | copy-start | bytes 122884
  71.9 6.8 %copy-start.22 = (bf16[160,1,128]{2,0,1:T(8,128)(2,1)S(1)}, bf16[160,1,128]{2,0,1:T(8,128)(2,1)}, u32[]{:S(2)}) copy-start(bf16[160,1,128]{2,0,1:T(8,128)(2,1)} %copy-done.21) | copy-start | bytes 122884
  71.9 6.8 %copy-start.24 = (bf16[160,1,128]{2,0,1:T(8,128)(2,1)S(1)}, bf16[160,1,128]{2,0,1:T(8,128)(2,1)}, u32[]{:S(2)}) copy-start(bf16[160,1,128]{2,0,1:T(8,128)(2,1)} %copy-done.23) | copy-start | bytes 122884
  71.9 6.8 %copy-start.26 = (bf16[160,1,128]{2,0,1:T(8,128)(2,1)S(1)}, bf16[160,1,128]{2,0,1:T(8,128)(2,1)}, u32[]{:S(2)}) copy-start(bf16[160,1,128]{2,0,1:T(8,128)(2,1)} %copy-done.25) | copy-start | bytes 122884
  75.3 5.3 %copy-start.38 = (f32[128,4]{0,1:T(4,128)S(1)}, f32[128,4]{0,1:T(4,128)}, u32[]{:S(2)}) copy-start(f32[128,4]{0,1:T(4,128)} %copy-done.37) | copy-start | bytes 6148
  75.3 5.3 %copy-start.43 = (f32[128]{0:T(128)S(1)}, f32[128]{0:T(128)}, u32[]{:S(2)}) copy-start(f32[128]{0:T(128)} %param.16) | copy-start | bytes 1540
  77.5 3.6 %copy-start.45 = (f32[128]{0:T(128)S(1)}, f32[128]{0:T(128)}, u32[]{:S(2)}) copy-start(f32[128]{0:T(128)} %param.15) | copy-start | bytes 1540
  84.7 2.0 %copy-start.1 = (bf16[128,4096]{0,1:T(8,128)(2,1)S(1)}, bf16[128,4096]{0,1:T(8,128)(2,1)}, u32[]{:S(2)}) copy-start(bf16[128,4096]{0,1:T(8,128)(2,1)} %copy-done) | copy-start | bytes 3145732
  84.7 2.1 %copy-start.34 = (f32[128,32]{0,1:T(8,128)S(1)}, f32[128,32]{0,1:T(8,128)}, u32[]{:S(2)}) copy-start(f32[128,32]{0,1:T(8,128)} %get-tuple-element.48) | copy-start | bytes 49156
  84.7 2.1 %copy-start.35 = (f32[4096]{0:T(1024)S(1)}, f32[4096]{0:T(1024)}, u32[]{:S(2)}) copy-start(f32[4096]{0:T(1024)} %broadcast_bitcast_fusion) | copy-start | bytes 49156
  86.8 2.3 %copy-start.42 = (f32[4,4]{1,0:T(4,128)S(1)}, f32[4,4]{1,0:T(4,128)}, u32[]{:S(2)}) copy-start(f32[4,4]{1,0:T(4,128)} %copy-done.41) | copy-start | bytes 196
  86.8 2.4 %copy-start.36 = (bf16[4,512]{1,0:T(4,128)(2,1)S(1)}, bf16[4,512]{1,0:T(4,128)(2,1)}, u32[]{:S(2)}) copy-start(bf16[4,512]{1,0:T(4,128)(2,1)} %param.12) | copy-start | bytes 12292
  86.8 2.3 %slice-start = ((bf16[160,4,128]{2,0,1:T(8,128)(2,1)}), bf16[128,4,128]{2,0,1:T(8,128)(2,1)S(1)}, s32[]{:S(2)}) async-start(bf16[160,4,128]{2,0,1:T(8,128)(2,1)} %maximum_convert_fusion), calls=%async_computation.1 | async-start | bytes 262144 | tf_op jit(solution)/shard_map/slice | solution.py:84
  89.0 4.2 %copy-start.46 = (u32[32]{0:T(128)S(1)}, u32[32]{0:T(128)}, u32[]{:S(2)}) copy-start(u32[32]{0:T(128)} %constant.31) | copy-start | bytes 388
  89.0 37.8 %copy-start.31 = (f32[4,4,128]{2,1,0:T(4,128)S(1)}, f32[4,4,128]{2,1,0:T(4,128)}, u32[]{:S(2)}) copy-start(f32[4,4,128]{2,1,0:T(4,128)} %copy-done.30) | copy-start | bytes 24580
  89.0 37.8 %copy-start.44 = (f32[128]{0:T(128)S(1)}, f32[128]{0:T(128)}, u32[]{:S(2)}) copy-start(f32[128]{0:T(128)} %param.16) | copy-start | bytes 1540
  89.0 77.5 %copy-start.33 = (f32[1,4,4,128]{3,2,1,0:T(4,128)S(1)}, f32[1,4,4,128]{3,2,1,0:T(4,128)}, u32[]{:S(2)}) copy-start(f32[1,4,4,128]{3,2,1,0:T(4,128)} %copy-done.32) | copy-start | bytes 24580
  89.0 77.5 %copy-start.40 = (f32[512]{0:T(512)S(1)}, f32[512]{0:T(512)}, u32[]{:S(2)}) copy-start(f32[512]{0:T(512)} %copy-done.39) | copy-start | bytes 6148
  (1 other events, 0.6 us)
Sparse Core Ops, SparseCore 0:
  72.0 53.4 all-reduce.4
where the time goes:
time: 176 us; the launch traced here: 175 us
  blocking collectives  59.1 us (34%)
  waiting for transfers between devices  31 us (18%)
  local copies, waits for them, and re-layouts  27.1 us (15%)
  matrix products  22.8 us (13%)
  other arithmetic  18.5 us (11%)
  between operations  16.1 us (9%)
    psum x1, blocking collectives, local(): lax.psum((gain_query, gain_comp + gain_prompt), ('dp', 'group'))  39.3 us
    unnamed x2, waiting for transfers between devices  31 us
    unnamed x108, local copies, waits for them, and re-layouts  17.3 us
    all_gather x1, blocking collectives, local(): lax.all_gather(pnorm.reshape(shard, HK * HD), 'group', axis=0, tiled=True)  10.6 us
    all_gather x1, blocking collectives, local(): lax.all_gather(prompt_value, 'group', axis=0, tiled=True)  9.25 us
    div x4, matrix products, head_grads(): dscore = (expo / totals * (dprob - delta)).astype(jnp.bfloat16)  8.01 us
    dot_general x4, matrix products, head_grads(): jnp.einsum('gck,kd->cgd', dscore, key_head, preferred_element_type=jnp.fl...  6.62 us
    reduce_sum x2, other arithmetic, norm_back(): jnp.mean(scaled * unit, axis=-1, keepdims=True)  3.73 us
  transfers between devices with their start and end apart: 1, of which 1 were waited for; matrix products, arithmetic and copies ran while one was open for 12% of the time, Pallas kernels for 0%

commit v1 on v0

--- a/solution.py
+++ b/solution.py
@@ -2,6 +2,7 @@
 import jax.numpy as jnp
 from jax import lax
 from jax.sharding import PartitionSpec as P
+from jax.lax import psum
 
 HD = 128
 HQ = 32
@@ -87,7 +88,7 @@
     dq, gain_query = norm_back(dquery, qunit, qinv, q_gain)
     dck, gain_comp = norm_back(dkey_comp, cunit, cinv, k_gain)
     dpk, gain_prompt = norm_back(dkey_prompt, punit, pinv, k_gain)
-    gain_query, gain_key = lax.psum((gain_query, gain_comp + gain_prompt), ("dp", "group"))
+    gain_query, gain_key = psum(psum((gain_query, gain_comp + gain_prompt), "group"), "dp")
     return (
         dq.reshape(count, HQ * HD).astype(jnp.bfloat16),
         dck.reshape(count, HK * HD).astype(jnp.bfloat16),

time: 176 us -> 160 us (0.909)
  blocking collectives: 59.1 us -> 43.8 us
    psum x1 -> x2, blocking collectives: 39.3 us -> 24 us  [the longest x1 12.2 us: local(): psum(psum((gain_query, gain_comp + gain_prompt), 'group'), 'dp')]
    unnamed x108 -> x104, local copies, waits for them, and re-layouts: 17.3 us -> 16.4 us
  transfers between devices with their start and end apart: 1 -> 1, of which waited for: 1 -> 1; matrix products, arithmetic and copies ran while one was open for 12% -> 14% of each run, Pallas kernels for 0% -> 0%
where the time goes in v1:
time: 160 us; the launch traced here: 159 us
  blocking collectives  43.8 us (27%)
  waiting for transfers between devices  31.1 us (19%)
  local copies, waits for them, and re-layouts  26.5 us (17%)
  matrix products  22.8 us (14%)
  other arithmetic  18.9 us (12%)
  between operations  16.1 us (10%)
    unnamed x2, waiting for transfers between devices  31.1 us
    unnamed x104, local copies, waits for them, and re-layouts  16.4 us
    psum x1, blocking collectives, local(): psum(psum((gain_query, gain_comp + gain_prompt), 'group'), 'dp')  12.2 us
    psum x1, blocking collectives, local(): psum((gain_query, gain_comp + gain_prompt), 'group')  11.8 us
    all_gather x1, blocking collectives, local(): lax.all_gather(pnorm.reshape(shard, HK * HD), 'group', axis=0, tiled=True)  10.6 us
    all_gather x1, blocking collectives, local(): lax.all_gather(prompt_value, 'group', axis=0, tiled=True)  9.25 us
    div x4, matrix products, head_grads(): dscore = (expo / totals * (dprob - delta)).astype(jnp.bfloat16)  7.97 us
    dot_general x4, matrix products, head_grads(): jnp.einsum('gck,kd->cgd', dscore, key_head, preferred_element_type=jnp.fl...  6.63 us
  transfers between devices with their start and end apart: 1, of which 1 were waited for; matrix products, arithmetic and copies ran while one was open for 14% of the time, Pallas kernels for 0%

profile of v1, /device:TPU:0, one launch (start us, length us, event | category | flops | bytes accessed | tf_op | source)
XLA Modules:
  0.0 159.3 jit_solution(5741649933149767077)
XLA Ops:
  7.2 0.6 iota_compare_fusion
  7.8 0.7 broadcast_bitcast_fusion.3
  8.5 0.7 reshape.176
  9.9 0.6 copy-done.32
  10.5 0.7 fusion.87
  11.2 10.6 %all-gather = bf16[8,4,512]{2,1,0:T(4,128)(2,1)S(1)} all-gather(bf16[1,4,512]{2,1,0:T(4,128)(2,1)S(1)} %fusion.87), channel_id=1, replica_groups=mesh['dp'=4,'group'=8] {'group'}, dimensions={0}, use_global_device_ids=true | all-gather | bytes 36864 | tf_op jit(solution)/shard_map/all_gather | solution.py:52
  21.8 0.6 copy.94
  22.4 1.0 copy.92
  23.8 0.7 copy.91
  24.7 0.7 add_rsqrt_fusion
  26.0 1.3 concatenate.21
  27.3 1.3 fusion.81
  28.6 1.4 multiply_convert_fusion
  30.0 2.0 %fusion.52 = f32[8,128,160]{1,2,0:T(8,128)} fusion(pred[128,160]{0,1:T(8,128)(4,1)} %concatenate.21, bf16[128,4,8,128]{3,0,2,1:T(8,128)(2,1)S(1)} %multiply_convert_fusion, bf16[128,4,128]{2,0,1:T(8,128)(2,1)S(1)} %copy.95, bf16[32,4,128]{2,0,1:T(8,128)(2,1)} %copy.94), kind=kOutput, calls=%fused_computation.88 | convolution fusion | flops 42517664 | bytes 1101824 | tf_op jit(solution)/shard_map/div | solution.py:36
  32.0 1.9 %fusion.54 = f32[8,128,160]{1,2,0:T(8,128)} fusion(pred[128,160]{0,1:T(8,128)(4,1)} %concatenate.21, bf16[128,4,8,128]{3,0,2,1:T(8,128)(2,1)S(1)} %multiply_convert_fusion, bf16[128,4,128]{2,0,1:T(8,128)(2,1)S(1)} %copy.95, bf16[32,4,128]{2,0,1:T(8,128)(2,1)} %copy.94), kind=kOutput, calls=%fused_computation.90 | convolution fusion | flops 42517664 | bytes 1101824 | tf_op jit(solution)/shard_map/div | solution.py:36
  33.9 1.9 %fusion.56 = f32[8,128,160]{1,2,0:T(8,128)} fusion(pred[128,160]{0,1:T(8,128)(4,1)} %concatenate.21, bf16[128,4,8,128]{3,0,2,1:T(8,128)(2,1)S(1)} %multiply_convert_fusion, bf16[128,4,128]{2,0,1:T(8,128)(2,1)S(1)} %copy.95, bf16[32,4,128]{2,0,1:T(8,128)(2,1)} %copy.94), kind=kOutput, calls=%fused_computation.92 | convolution fusion | flops 42517664 | bytes 1101824 | tf_op jit(solution)/shard_map/div | solution.py:36
  37.0 9.3 %all-gather.1 = bf16[8,4,512]{2,1,0:T(4,128)(2,1)S(1)} all-gather(bf16[1,4,512]{2,1,0:T(4,128)(2,1)} %bitcast.375), channel_id=1, replica_groups=mesh['dp'=4,'group'=8] {'group'}, dimensions={0}, use_global_device_ids=true | all-gather | bytes 36864 | tf_op jit(solution)/shard_map/all_gather | solution.py:53
  46.3 0.9 pad_maximum_fusion.2
  47.2 0.9 fusion.122
  48.2 2.3 %copy.98 = bf16[128,4096]{0,1:T(8,128)(2,1)} copy(bf16[128,4096]{1,0:T(8,128)(2,1)} %param.14) | data formatting | bytes 2097152 | tf_op args[5]
  50.5 1.3 broadcast_select_fusion
  51.8 1.0 fusion.121
  52.8 1.8 %copy.133 = bf16[128,1,8,128]{3,0,2,1:T(8,128)(2,1)} copy(bf16[128,1,8,128]{0,3,2,1:T(8,128)(2,1)} %get-tuple-element.40) | data formatting | bytes 524288
  54.6 1.8 %copy.137 = bf16[128,1,8,128]{3,0,2,1:T(8,128)(2,1)} copy(bf16[128,1,8,128]{0,3,2,1:T(8,128)(2,1)} %get-tuple-element.41) | data formatting | bytes 524288
  56.4 1.8 %copy.135 = bf16[128,1,8,128]{3,0,2,1:T(8,128)(2,1)} copy(bf16[128,1,8,128]{0,3,2,1:T(8,128)(2,1)} %get-tuple-element.42) | data formatting | bytes 524288
  58.2 1.8 %copy.139 = bf16[128,1,8,128]{3,0,2,1:T(8,128)(2,1)} copy(bf16[128,1,8,128]{0,3,2,1:T(8,128)(2,1)} %get-tuple-element.43) | data formatting | bytes 524288
  59.9 2.1 %fusion.50 = f32[8,128,160]{1,2,0:T(8,128)} fusion(bf16[160,128,1]{1,0,2:T(8,128)(2,1)} %fusion.81, pred[128,160]{0,1:T(8,128)(4,1)} %concatenate.21, bf16[128,4,8,128]{3,0,2,1:T(8,128)(2,1)} %copy-done.6), kind=kOutput, calls=%fused_computation.86 | convolution fusion | flops 42435744 | bytes 978944 | tf_op jit(solution)/shard_map/div | solution.py:36
  62.1 1.5 convolution_bitcast_fusion.8
  63.6 1.7 %fusion.37 = f32[128,8]{0,1:T(8,128)S(1)} fusion(bf16[128,1,8,128]{3,0,2,1:T(8,128)(2,1)} %copy.139, f32[8,128,160]{1,2,0:T(8,128)} %fusion.50, bf16[160,1,128]{2,1,0:T(2,128)(2,1)} %get-tuple-element.47), kind=kOutput, calls=%fused_computation.62 | convolution fusion | flops 42499072 | bytes 962560 | tf_op jit(solution)/shard_map/gck,kd->cgd/dot_general | solution.py:33
  65.3 1.1 fusion.36
  71.1 0.6 pad_maximum_fusion.3
  71.8 0.7 broadcast_bitcast_fusion
  72.5 2.1 %fusion.29 = f32[128,1,8,128]{3,0,2,1:T(8,128)} fusion(bf16[160,128,1]{1,0,2:T(8,128)(2,1)} %fusion.81, bf16[8,128,160]{1,2,0:T(8,128)(2,1)} %copy-done.8), kind=kOutput, calls=%fused_computation.51 | convolution fusion | flops 42074112 | bytes 892928 | tf_op jit(solution)/shard_map/gck,kd->cgd/dot_general | solution.py:37
  74.7 2.2 %fusion.30 = f32[128,1,8,128]{3,0,2,1:T(8,128)} fusion(bf16[8,128,160]{1,2,0:T(8,128)(2,1)} %copy-done.9, bf16[128,4,128]{2,0,1:T(8,128)(2,1)S(1)} %copy.95, bf16[32,4,128]{2,0,1:T(8,128)(2,1)} %copy.94), kind=kOutput, calls=%fused_computation.53 | convolution fusion | flops 42156032 | bytes 1015808 | tf_op jit(solution)/shard_map/gck,kd->cgd/dot_general | solution.py:37
  76.9 1.2 fusion.31
  78.1 0.7 maximum_convert_fusion
  78.7 1.1 fusion.32
  80.5 3.5 %multiply_reduce_fusion = (f32[128,4,8]{0,2,1:T(8,128)S(1)}, f32[128,4,8,128]{3,0,2,1:T(8,128)}) fusion(f32[128,4,8,128]{3,0,2,1:T(8,128)S(1)} %copy.96, f32[128]{0:T(128)S(1)} %copy-done.43, f32[128,4,8]{0,2,1:T(8,128)S(1)} %get-tuple-element.51, f32[128,1,8,128]{3,0,2,1:T(8,128)} %fusion.29, f32[128,1,8,128]{3,0,2,1:T(8,128)} %fusion.30, ...), kind=kLoop, calls=%fused_computation.11 | loop fusion | flops 3665920 | bytes 6324736 | tf_op jit(solution)/shard_map/reduce_sum | solution.py:22
  84.1 3.0 %copy.114 = f32[128,4,8,128]{0,3,2,1:T(8,128)} copy(f32[128,4,8,128]{3,0,2,1:T(8,128)} %get-tuple-element.39) | data formatting | bytes 4194304 | tf_op jit(solution)/shard_map/stack | solution.py:71
  87.1 2.6 %fusion.4 = (f32[4096]{0:T(1024)S(1)}, bf16[128,4096]{0,1:T(8,128)(2,1)S(1)}) fusion(f32[128,4,8,128]{0,3,2,1:T(8,128)} %copy.114, bf16[128,4096]{0,1:T(8,128)(2,1)S(1)} %copy-done.1, f32[128,4,8]{0,2,1:T(8,128)S(1)} %get-tuple-element.51, f32[128,32]{0,1:T(8,128)S(1)} %multiply_bitcast_fusion, f32[4096]{0:T(1024)S(1)} %broadcast_bitcast_fusion, ...), kind=kLoop, calls=%fused_computation.8 | loop fusion | flops 5238784 | bytes 4276224 | tf_op jit(solution)/shard_map/reduce_sum | solution.py:23
  90.0 0.8 copy.123
  91.0 0.8 copy.122
  91.7 1.3 copy.121
  94.3 31.1 %all-reduce.6.cloned.1.call-done = bf16[32,1024]{1,0:T(8,128)(2,1)} async-done(((bf16[32,1024]{1,0:T(8,128)(2,1)}), bf16[32,1024]{1,0:T(8,128)(2,1)}) %all-reduce.6.cloned.1.call-update) | async-done | bytes 65552
  125.4 1.4 fusion.123
  127.1 11.8 %all-reduce.2 = (f32[128]{0:T(128)S(1)}, f32[128]{0:T(128)S(1)}) all-reduce(f32[128]{0:T(128)S(1)} %bitcast_reduce_fusion.1, f32[128]{0:T(128)S(1)} %add.52), channel_id=1, replica_groups=mesh['dp'=4,'group'=8] {'group'}, use_global_device_ids=true, to_apply=%region_17.18 | all-reduce | flops 256 | bytes 2048 | tf_op jit(solution)/shard_map/psum | solution.py:91
  138.9 12.2 %all-reduce.3 = (f32[128]{0:T(128)}, f32[128]{0:T(128)}) all-reduce(f32[128]{0:T(128)S(1)} %get-tuple-element.30, f32[128]{0:T(128)S(1)} %get-tuple-element.31), channel_id=1, replica_groups=mesh['dp'=4,'group'=8] {'dp'}, use_global_device_ids=true, to_apply=%region_18.19 | all-reduce | flops 256 | bytes 2048 | tf_op jit(solution)/shard_map/psum | solution.py:91
  151.1 1.3 fusion.86
  (139 shorter events, 8.8 us)
Async XLA Ops:
  7.2 16.6 %copy-start.14 = (bf16[128,4096]{1,0:T(8,128)(2,1)S(1)}, bf16[128,4096]{1,0:T(8,128)(2,1)}, u32[]{:S(2)}) copy-start(bf16[128,4096]{1,0:T(8,128)(2,1)} %param.9) | copy-start | bytes 3145732
  7.2 118.2 %all-reduce.6.cloned.1.call-start = ((), (), s32[]{:S(2)}) async-start(), calls=%async_computation | async-start | bytes 131072
  8.5 16.2 %copy-start.38 = (f32[512]{0:T(512)}, f32[512]{0:T(512)S(1)}, u32[]{:S(2)}) copy-start(f32[512]{0:T(512)S(1)} %broadcast_bitcast_fusion.3) | copy-start | bytes 6148
  9.2 0.6 copy-start.30
  9.3 0.6 copy-start.40
  9.9 0.6 copy-start.32
  23.5 2.0 %copy-start.36 = (f32[128,4]{0,1:T(4,128)}, f32[128,4]{0,1:T(4,128)S(1)}, u32[]{:S(2)}) copy-start(f32[128,4]{0,1:T(4,128)S(1)} %add_rsqrt_fusion.1) | copy-start | bytes 6148
  24.4 1.5 copy-start
  30.0 3.9 %copy-start.6 = (bf16[128,4,8,128]{3,0,2,1:T(8,128)(2,1)}, bf16[128,4,8,128]{3,0,2,1:T(8,128)(2,1)S(1)}, u32[]{:S(2)}) copy-start(bf16[128,4,8,128]{3,0,2,1:T(8,128)(2,1)S(1)} %multiply_convert_fusion) | copy-start | bytes 3145732
  62.1 3.2 %copy-start.5 = (f32[8,128,160]{1,2,0:T(8,128)S(1)}, f32[8,128,160]{1,2,0:T(8,128)}, u32[]{:S(2)}) copy-start(f32[8,128,160]{1,2,0:T(8,128)} %fusion.50) | copy-start | bytes 1966084
  62.1 4.4 %copy-start.7 = (bf16[128,4,8,128]{3,0,2,1:T(8,128)(2,1)S(1)}, bf16[128,4,8,128]{3,0,2,1:T(8,128)(2,1)}, u32[]{:S(2)}) copy-start(bf16[128,4,8,128]{3,0,2,1:T(8,128)(2,1)} %copy-done.6) | copy-start | bytes 3145732
  62.1 4.6 %copy-start.4 = (f32[8,128,160]{1,2,0:T(8,128)S(1)}, f32[8,128,160]{1,2,0:T(8,128)}, u32[]{:S(2)}) copy-start(f32[8,128,160]{1,2,0:T(8,128)} %fusion.52) | copy-start | bytes 1966084
  63.5 7.1 %copy-start.19 = (bf16[160,1,128]{2,0,1:T(8,128)(2,1)}, bf16[160,1,128]{2,0,1:T(8,128)(2,1)S(1)}, u32[]{:S(2)}) copy-start(bf16[160,1,128]{2,0,1:T(8,128)(2,1)S(1)} %convolution_bitcast_fusion.8) | copy-start | bytes 122884
  63.6 3.4 %copy-start.17 = (bf16[128,1,8,128]{3,0,2,1:T(8,128)(2,1)S(1)}, bf16[128,1,8,128]{3,0,2,1:T(8,128)(2,1)}, u32[]{:S(2)}) copy-start(bf16[128,1,8,128]{3,0,2,1:T(8,128)(2,1)} %copy.137) | copy-start | bytes 786436
  63.6 3.4 %copy-start.29 = (bf16[160,1,128]{2,1,0:T(2,128)(2,1)S(1)}, bf16[160,1,128]{2,1,0:T(2,128)(2,1)}, u32[]{:S(2)}) copy-start(bf16[160,1,128]{2,1,0:T(2,128)(2,1)} %get-tuple-element.45) | copy-start | bytes 122884
  66.4 1.6 copy-start.8
  66.7 1.3 copy-start.3
  67.0 3.7 %copy-start.21 = (bf16[160,1,128]{2,0,1:T(8,128)(2,1)}, bf16[160,1,128]{2,0,1:T(8,128)(2,1)S(1)}, u32[]{:S(2)}) copy-start(bf16[160,1,128]{2,0,1:T(8,128)(2,1)S(1)} %convolution_bitcast_fusion.9) | copy-start | bytes 122884
  67.0 1.4 copy-start.16
  67.0 1.4 copy-start.28
  67.8 1.6 copy-start.9
  68.0 1.3 copy-start.2
  68.3 2.4 %copy-start.23 = (bf16[160,1,128]{2,0,1:T(8,128)(2,1)}, bf16[160,1,128]{2,0,1:T(8,128)(2,1)S(1)}, u32[]{:S(2)}) copy-start(bf16[160,1,128]{2,0,1:T(8,128)(2,1)S(1)} %convolution_bitcast_fusion.10) | copy-start | bytes 122884
  68.3 1.3 copy-start.15
  68.3 1.3 copy-start.27
  69.1 1.6 copy-start.10
  69.6 1.5 copy-start.25
  70.4 0.7 copy-start.12
  70.4 6.5 %copy-start.18 = (bf16[32,4,128]{2,0,1:T(8,128)(2,1)S(1)}, bf16[32,4,128]{2,0,1:T(8,128)(2,1)}, u32[]{:S(2)}) copy-start(bf16[32,4,128]{2,0,1:T(8,128)(2,1)} %copy.94) | copy-start | bytes 98308
  71.1 5.7 %copy-start.11 = (bf16[8,128,160]{1,2,0:T(8,128)(2,1)S(1)}, bf16[8,128,160]{1,2,0:T(8,128)(2,1)}, u32[]{:S(2)}) copy-start(bf16[8,128,160]{1,2,0:T(8,128)(2,1)} %copy-done.10) | copy-start | bytes 983044
  71.1 7.6 %copy-start.13 = (bf16[8,128,160]{1,2,0:T(8,128)(2,1)S(1)}, bf16[8,128,160]{1,2,0:T(8,128)(2,1)}, u32[]{:S(2)}) copy-start(bf16[8,128,160]{1,2,0:T(8,128)(2,1)} %copy-done.12) | copy-start | bytes 983044
  71.8 6.2 %copy-start.20 = (bf16[160,1,128]{2,0,1:T(8,128)(2,1)S(1)}, bf16[160,1,128]{2,0,1:T(8,128)(2,1)}, u32[]{:S(2)}) copy-start(bf16[160,1,128]{2,0,1:T(8,128)(2,1)} %copy-done.19) | copy-start | bytes 122884
  71.8 6.2 %copy-start.22 = (bf16[160,1,128]{2,0,1:T(8,128)(2,1)S(1)}, bf16[160,1,128]{2,0,1:T(8,128)(2,1)}, u32[]{:S(2)}) copy-start(bf16[160,1,128]{2,0,1:T(8,128)(2,1)} %copy-done.21) | copy-start | bytes 122884
  71.8 6.2 %copy-start.24 = (bf16[160,1,128]{2,0,1:T(8,128)(2,1)S(1)}, bf16[160,1,128]{2,0,1:T(8,128)(2,1)}, u32[]{:S(2)}) copy-start(bf16[160,1,128]{2,0,1:T(8,128)(2,1)} %copy-done.23) | copy-start | bytes 122884
  71.8 6.2 %copy-start.26 = (bf16[160,1,128]{2,0,1:T(8,128)(2,1)S(1)}, bf16[160,1,128]{2,0,1:T(8,128)(2,1)}, u32[]{:S(2)}) copy-start(bf16[160,1,128]{2,0,1:T(8,128)(2,1)} %copy-done.25) | copy-start | bytes 122884
  74.7 5.3 %copy-start.37 = (f32[128,4]{0,1:T(4,128)S(1)}, f32[128,4]{0,1:T(4,128)}, u32[]{:S(2)}) copy-start(f32[128,4]{0,1:T(4,128)} %copy-done.36) | copy-start | bytes 6148
  74.7 5.3 %copy-start.42 = (f32[128]{0:T(128)S(1)}, f32[128]{0:T(128)}, u32[]{:S(2)}) copy-start(f32[128]{0:T(128)} %param.16) | copy-start | bytes 1540
  76.9 3.6 %copy-start.43 = (f32[128]{0:T(128)S(1)}, f32[128]{0:T(128)}, u32[]{:S(2)}) copy-start(f32[128]{0:T(128)} %param.15) | copy-start | bytes 1540
  84.1 3.0 %copy-start.1 = (bf16[128,4096]{0,1:T(8,128)(2,1)S(1)}, bf16[128,4096]{0,1:T(8,128)(2,1)}, u32[]{:S(2)}) copy-start(bf16[128,4096]{0,1:T(8,128)(2,1)} %copy-done) | copy-start | bytes 3145732
  84.1 3.0 %copy-start.34 = (f32[128,32]{0,1:T(8,128)S(1)}, f32[128,32]{0,1:T(8,128)}, u32[]{:S(2)}) copy-start(f32[128,32]{0,1:T(8,128)} %get-tuple-element.50) | copy-start | bytes 49156
  87.1 2.7 %copy-start.41 = (f32[4,4]{1,0:T(4,128)S(1)}, f32[4,4]{1,0:T(4,128)}, u32[]{:S(2)}) copy-start(f32[4,4]{1,0:T(4,128)} %copy-done.40) | copy-start | bytes 196
  87.1 2.8 %copy-start.35 = (bf16[4,512]{1,0:T(4,128)(2,1)S(1)}, bf16[4,512]{1,0:T(4,128)(2,1)}, u32[]{:S(2)}) copy-start(bf16[4,512]{1,0:T(4,128)(2,1)} %param.12) | copy-start | bytes 12292
  87.1 2.8 %slice-start = ((bf16[160,4,128]{2,0,1:T(8,128)(2,1)}), bf16[128,4,128]{2,0,1:T(8,128)(2,1)S(1)}, s32[]{:S(2)}) async-start(bf16[160,4,128]{2,0,1:T(8,128)(2,1)} %maximum_convert_fusion), calls=%async_computation.1 | async-start | bytes 262144 | tf_op jit(solution)/shard_map/slice | solution.py:85
  89.7 3.3 %copy-start.44 = (u32[32]{0:T(128)S(1)}, u32[32]{0:T(128)}, u32[]{:S(2)}) copy-start(u32[32]{0:T(128)} %constant.31) | copy-start | bytes 388
  89.7 37.1 %copy-start.31 = (f32[4,4,128]{2,1,0:T(4,128)S(1)}, f32[4,4,128]{2,1,0:T(4,128)}, u32[]{:S(2)}) copy-start(f32[4,4,128]{2,1,0:T(4,128)} %copy-done.30) | copy-start | bytes 24580
  89.8 61.4 %copy-start.33 = (f32[1,4,4,128]{3,2,1,0:T(4,128)S(1)}, f32[1,4,4,128]{3,2,1,0:T(4,128)}, u32[]{:S(2)}) copy-start(f32[1,4,4,128]{3,2,1,0:T(4,128)} %copy-done.32) | copy-start | bytes 24580
  89.8 61.4 %copy-start.39 = (f32[512]{0:T(512)S(1)}, f32[512]{0:T(512)}, u32[]{:S(2)}) copy-start(f32[512]{0:T(512)} %copy-done.38) | copy-start | bytes 6148
Sparse Core Ops, SparseCore 0:
  71.9 53.4 all-reduce.5
